TPU v7x, 32 devices: a whole 2x2x4 slice. The times are simulated.
32 devices in a mesh: rep: 16 (over z, y, core), grp: 2 (over x).
Axes of the slice: x: 2, y: 2, z: 4, core: 2. Of those that a mesh axis runs over, the one named last changes fastest.
Arguments:
- tokens: bfloat16 [16, 1568, 1024], P('rep', 'grp'), may hold values from -6 to 6
- query_weight: bfloat16 [1024, 1024], P('grp'), may hold values from -0.1875 to 0.1875
- key_weight: bfloat16 [1024, 1024], P('grp'), may hold values from -0.1875 to 0.1875
- value_weight: bfloat16 [1024, 1024], P('grp'), may hold values from -0.1875 to 0.1875
- query_bias: float32 [1024], P('grp'), may hold values from -4 to 4
- value_bias: float32 [1024], P('grp'), may hold values from -0.75 to 0.75
- out_weight: bfloat16 [1024, 1024], P('grp'), may hold values from -4 to 4
- out_bias: float32 [1024], P('grp'), may hold values from -4 to 4
- first_gain: float32 [1024], P('grp'), may hold values from 0.5 to 1.5
- first_shift: float32 [1024], P('grp'), may hold values from -4 to 4
- second_gain: float32 [1024], P('grp'), may hold values from 0.5 to 1.5
- second_shift: float32 [1024], P('grp'), may hold values from -4 to 4
- up_weight: bfloat16 [1024, 4096], P('grp'), may hold values from -0.1875 to 0.1875
- up_bias: float32 [4096], P('grp'), may hold values from -4 to 4
- down_weight: bfloat16 [4096, 1024], P('grp'), may hold values from -0.09375 to 0.09375
- down_bias: float32 [1024], P('grp'), may hold values from -4 to 4
- cotangent: bfloat16 [16, 1568, 1024], P('rep', 'grp'), may hold values from -6 to 6
Outputs:
- layer_out: bfloat16 [16, 1568, 1024], P('rep', 'grp')
- tokens_grad: bfloat16 [16, 1568, 1024], P('rep', 'grp')
- query_weight_grad: float32 [1024, 1024], P('grp')
- key_weight_grad: float32 [1024, 1024], P('grp')
- value_weight_grad: float32 [1024, 1024], P('grp')
- query_bias_grad: float32 [1024], P('grp')
- value_bias_grad: float32 [1024], P('grp')
- out_weight_grad: float32 [1024, 1024], P('grp')
- out_bias_grad: float32 [1024], P('grp')
- first_gain_grad: float32 [1024], P('grp')
- first_shift_grad: float32 [1024], P('grp')
- second_gain_grad: float32 [1024], P('grp')
- second_shift_grad: float32 [1024], P('grp')
- up_weight_grad: float32 [1024, 4096], P('grp')
- up_bias_grad: float32 [4096], P('grp')
- down_weight_grad: float32 [4096, 1024], P('grp')
- down_bias_grad: float32 [1024], P('grp')
All inputs are finite; a program needn't handle non-finite values.
Results may differ from a plain program's by a relative error of at most 0.033.
Values may be sent and summed in bfloat16 or wider, within the bound.
No kernel may reach another device: no remote copies, remote signals or barrier semaphores. Data moves between devices by JAX's collectives and lax.ppermute only.
A program may use at most 448 MiB of HBM per device.

v0:
```python
from functools import partial

import jax
import jax.numpy as jnp
from jax import lax
from jax.sharding import PartitionSpec as P

HEAD_DIM = 64


EPS = 1e-06


def norm_parts(values, gain, shift):
    average = jnp.mean(values, axis=-1, keepdims=True)
    centred = values - average
    spread = jnp.mean(centred * centred, axis=-1, keepdims=True)
    inverse = lax.rsqrt(spread + EPS)
    normed = centred * inverse
    return (normed * gain + shift, normed, inverse)


def norm_back(grad, normed, inverse, gain):
    scaled = grad * gain
    first_term = jnp.mean(scaled, axis=-1, keepdims=True)
    second_term = jnp.mean(scaled * normed, axis=-1, keepdims=True)
    result = inverse * (scaled - first_term - normed * second_term)
    return (result, jnp.sum(grad * normed, axis=0), jnp.sum(grad, axis=0))


def matmul(left, right):
    return jnp.dot(left, right, preferred_element_type=jnp.float32)


def matmul_right_t(left, right):
    return lax.dot_general(
        left, right, (((1,), (1,)), ((), ())), preferred_element_type=jnp.float32
    )


def matmul_left_t(left, right):
    return lax.dot_general(
        left, right, (((0,), (0,)), ((), ())), preferred_element_type=jnp.float32
    )


def split_heads(values):
    return values.reshape(values.shape[0], values.shape[1] // HEAD_DIM, HEAD_DIM)


def attend_clip(operands):
    queries, keys, values = operands
    scale = HEAD_DIM ** (-0.5)
    scores = (
        jnp.einsum(
            "qhd,khd->hqk",
            split_heads(queries),
            split_heads(keys),
            preferred_element_type=jnp.float32,
        )
        * scale
    )
    highest = jnp.max(scores, axis=-1, keepdims=True)
    expon = jnp.exp(scores - highest)
    totals = jnp.sum(expon, axis=-1, keepdims=True)
    probs = (expon / totals).astype(jnp.bfloat16)
    mixed = jnp.einsum(
        "hqk,khd->qhd", probs, split_heads(values), preferred_element_type=jnp.float32
    )
    return (
        mixed.reshape(queries.shape[0], queries.shape[1]),
        highest[..., 0] + jnp.log(totals[..., 0]),
    )


def attend_back(operands):
    queries, keys, values, grad_mixed, log_total = operands
    scale = HEAD_DIM ** (-0.5)
    query_heads = split_heads(queries)
    key_heads = split_heads(keys)
    grad_heads = split_heads(grad_mixed)
    scores = (
        jnp.einsum("qhd,khd->hqk", query_heads, key_heads, preferred_element_type=jnp.float32)
        * scale
    )
    weights = jnp.exp(scores - log_total[..., None])
    probs = weights.astype(jnp.bfloat16)
    grad_probs = jnp.einsum(
        "qhd,khd->hqk", grad_heads, split_heads(values), preferred_element_type=jnp.float32
    )
    grad_values = jnp.einsum("hqk,qhd->khd", probs, grad_heads, preferred_element_type=jnp.float32)
    inner = jnp.sum(grad_probs * weights, axis=-1, keepdims=True)
    grad_scores = (weights * (grad_probs - inner)).astype(jnp.bfloat16)
    grad_queries = (
        jnp.einsum("hqk,khd->qhd", grad_scores, key_heads, preferred_element_type=jnp.float32)
        * scale
    )
    grad_keys = (
        jnp.einsum("hqk,qhd->khd", grad_scores, query_heads, preferred_element_type=jnp.float32)
        * scale
    )
    return (
        grad_queries.reshape(queries.shape[0], queries.shape[1]),
        grad_keys.reshape(keys.shape[0], keys.shape[1]),
        grad_values.reshape(keys.shape[0], keys.shape[1]),
    )


def body(
    tokens,
    query_weight,
    key_weight,
    value_weight,
    query_bias,
    value_bias,
    out_weight,
    out_bias,
    first_gain,
    first_shift,
    second_gain,
    second_shift,
    up_weight,
    up_bias,
    down_weight,
    down_bias,
    cotangent,
):
    clips, local_len, width = tokens.shape
    rows = clips * local_len
    attention_set = (
        lax.all_gather(query_weight, "grp", axis=0, tiled=True),
        lax.all_gather(key_weight, "grp", axis=0, tiled=True),
        lax.all_gather(value_weight, "grp", axis=0, tiled=True),
        lax.all_gather(query_bias.astype(jnp.bfloat16), "grp", axis=0, tiled=True).astype(
            query_bias.dtype
        ),
        lax.all_gather(value_bias.astype(jnp.bfloat16), "grp", axis=0, tiled=True).astype(
            value_bias.dtype
        ),
        lax.all_gather(out_weight, "grp", axis=0, tiled=True),
        lax.all_gather(out_bias.astype(jnp.bfloat16), "grp", axis=0, tiled=True).astype(
            out_bias.dtype
        ),
        lax.all_gather(first_gain.astype(jnp.bfloat16), "grp", axis=0, tiled=True).astype(
            first_gain.dtype
        ),
        lax.all_gather(first_shift.astype(jnp.bfloat16), "grp", axis=0, tiled=True).astype(
            first_shift.dtype
        ),
    )
    feed_set = (
        lax.all_gather(second_gain.astype(jnp.bfloat16), "grp", axis=0, tiled=True).astype(
            second_gain.dtype
        ),
        lax.all_gather(second_shift.astype(jnp.bfloat16), "grp", axis=0, tiled=True).astype(
            second_shift.dtype
        ),
        lax.all_gather(up_weight, "grp", axis=0, tiled=True),
        lax.all_gather(up_bias.astype(jnp.bfloat16), "grp", axis=0, tiled=True).astype(
            up_bias.dtype
        ),
        lax.all_gather(down_weight, "grp", axis=0, tiled=True),
        lax.all_gather(down_bias.astype(jnp.bfloat16), "grp", axis=0, tiled=True).astype(
            down_bias.dtype
        ),
    )
    (
        full_query,
        full_key,
        full_value,
        full_qbias,
        full_vbias,
        full_out,
        full_obias,
        full_gain_one,
        full_shift_one,
    ) = attention_set
    full_gain_two, full_shift_two, full_up, full_ubias, full_down, full_dbias = feed_set
    inputs = tokens.reshape(rows, width).astype(jnp.float32)
    first_norm, first_normed, first_inverse = norm_parts(inputs, full_gain_one, full_shift_one)
    first_low = first_norm.astype(jnp.bfloat16)
    query_low = (matmul(first_low, full_query) + full_qbias).astype(jnp.bfloat16)
    key_low = matmul(first_low, full_key).astype(jnp.bfloat16)
    value_low = (matmul(first_low, full_value) + full_vbias).astype(jnp.bfloat16)
    query_clips = query_low.reshape(clips, local_len, width)
    key_clips = key_low.reshape(clips, local_len, width)
    value_clips = value_low.reshape(clips, local_len, width)
    key_whole, value_whole = (
        lax.all_gather(key_clips, "grp", axis=1, tiled=True),
        lax.all_gather(value_clips, "grp", axis=1, tiled=True),
    )
    mixed, log_total = lax.map(attend_clip, (query_clips, key_whole, value_whole))
    mixed_low = mixed.reshape(rows, width).astype(jnp.bfloat16)
    middle = inputs + matmul(mixed_low, full_out) + full_obias
    second_norm, second_normed, second_inverse = norm_parts(middle, full_gain_two, full_shift_two)
    second_low = second_norm.astype(jnp.bfloat16)
    hidden_pre = matmul(second_low, full_up) + full_ubias
    hidden_low = jax.nn.gelu(hidden_pre, approximate=False).astype(jnp.bfloat16)
    result = middle + matmul(hidden_low, full_down) + full_dbias
    layer_out = result.astype(jnp.bfloat16).reshape(clips, local_len, width)
    attention_back = (
        lax.all_gather(query_weight, "grp", axis=0, tiled=True),
        lax.all_gather(key_weight, "grp", axis=0, tiled=True),
        lax.all_gather(value_weight, "grp", axis=0, tiled=True),
        lax.all_gather(query_bias.astype(jnp.bfloat16), "grp", axis=0, tiled=True).astype(
            query_bias.dtype
        ),
        lax.all_gather(value_bias.astype(jnp.bfloat16), "grp", axis=0, tiled=True).astype(
            value_bias.dtype
        ),
        lax.all_gather(out_weight, "grp", axis=0, tiled=True),
        lax.all_gather(out_bias.astype(jnp.bfloat16), "grp", axis=0, tiled=True).astype(
            out_bias.dtype
        ),
        lax.all_gather(first_gain.astype(jnp.bfloat16), "grp", axis=0, tiled=True).astype(
            first_gain.dtype
        ),
        lax.all_gather(first_shift.astype(jnp.bfloat16), "grp", axis=0, tiled=True).astype(
            first_shift.dtype
        ),
    )
    feed_back = (
        lax.all_gather(second_gain.astype(jnp.bfloat16), "grp", axis=0, tiled=True).astype(
            second_gain.dtype
        ),
        lax.all_gather(second_shift.astype(jnp.bfloat16), "grp", axis=0, tiled=True).astype(
            second_shift.dtype
        ),
        lax.all_gather(up_weight, "grp", axis=0, tiled=True),
        lax.all_gather(up_bias.astype(jnp.bfloat16), "grp", axis=0, tiled=True).astype(
            up_bias.dtype
        ),
        lax.all_gather(down_weight, "grp", axis=0, tiled=True),
        lax.all_gather(down_bias.astype(jnp.bfloat16), "grp", axis=0, tiled=True).astype(
            down_bias.dtype
        ),
    )
    (
        back_query,
        back_key,
        back_value,
        unused_qbias,
        unused_vbias,
        back_out,
        unused_obias,
        back_gain_one,
        unused_shift_one,
    ) = attention_back
    back_gain_two, unused_shift_two, back_up, unused_ubias, back_down, unused_dbias = feed_back
    grad_out = cotangent.reshape(rows, width)
    grad_out_wide = grad_out.astype(jnp.float32)
    grad_hidden = matmul_right_t(grad_out, back_down)
    grad_down_weight = matmul_left_t(hidden_low, grad_out)
    grad_down_bias = jnp.sum(grad_out_wide, axis=0)
    unused_value, gelu_pull = jax.vjp(partial(jax.nn.gelu, approximate=False), hidden_pre)
    grad_pre_low = gelu_pull(grad_hidden)[0].astype(jnp.bfloat16)
    grad_up_weight = matmul_left_t(second_low, grad_pre_low)
    grad_up_bias = jnp.sum(grad_pre_low.astype(jnp.float32), axis=0)
    grad_second, grad_gain_two, grad_shift_two = norm_back(
        matmul_right_t(grad_pre_low, back_up), second_normed, second_inverse, back_gain_two
    )
    grad_middle = grad_out_wide + grad_second
    grad_middle_low = grad_middle.astype(jnp.bfloat16)
    grad_out_weight = matmul_left_t(mixed_low, grad_middle_low)
    grad_out_bias = jnp.sum(grad_middle_low.astype(jnp.float32), axis=0)
    grad_mixed_low = matmul_right_t(grad_middle_low, back_out).astype(jnp.bfloat16)
    grad_mixed_clips = grad_mixed_low.reshape(clips, local_len, width)
    grad_queries, grad_keys, grad_values = lax.map(
        attend_back, (query_clips, key_whole, value_whole, grad_mixed_clips, log_total)
    )
    key_share, value_share = (
        lax.psum_scatter(
            grad_keys.astype(jnp.bfloat16), "grp", scatter_dimension=1, tiled=True
        ).astype(jnp.float32),
        lax.psum_scatter(
            grad_values.astype(jnp.bfloat16), "grp", scatter_dimension=1, tiled=True
        ).astype(jnp.float32),
    )
    query_grad_low = grad_queries.reshape(rows, width).astype(jnp.bfloat16)
    key_grad_low = key_share.reshape(rows, width).astype(jnp.bfloat16)
    value_grad_low = value_share.reshape(rows, width).astype(jnp.bfloat16)
    grad_query_weight = matmul_left_t(first_low, query_grad_low)
    grad_key_weight = matmul_left_t(first_low, key_grad_low)
    grad_value_weight = matmul_left_t(first_low, value_grad_low)
    grad_query_bias = jnp.sum(query_grad_low.astype(jnp.float32), axis=0)
    grad_value_bias = jnp.sum(value_grad_low.astype(jnp.float32), axis=0)
    grad_first_norm = (
        matmul_right_t(query_grad_low, back_query)
        + matmul_right_t(key_grad_low, back_key)
        + matmul_right_t(value_grad_low, back_value)
    )
    grad_first, grad_gain_one, grad_shift_one = norm_back(
        grad_first_norm, first_normed, first_inverse, back_gain_one
    )
    tokens_grad = (grad_middle + grad_first).astype(jnp.bfloat16).reshape(clips, local_len, width)
    shares = (
        lax.psum_scatter(
            grad_query_weight.astype(jnp.bfloat16), "grp", scatter_dimension=0, tiled=True
        ).astype(jnp.float32),
        lax.psum_scatter(
            grad_key_weight.astype(jnp.bfloat16), "grp", scatter_dimension=0, tiled=True
        ).astype(jnp.float32),
        lax.psum_scatter(
            grad_value_weight.astype(jnp.bfloat16), "grp", scatter_dimension=0, tiled=True
        ).astype(jnp.float32),
        lax.psum_scatter(
            grad_query_bias.astype(jnp.bfloat16), "grp", scatter_dimension=0, tiled=True
        ).astype(jnp.float32),
        lax.psum_scatter(
            grad_value_bias.astype(jnp.bfloat16), "grp", scatter_dimension=0, tiled=True
        ).astype(jnp.float32),
        lax.psum_scatter(
            grad_out_weight.astype(jnp.bfloat16), "grp", scatter_dimension=0, tiled=True
        ).astype(jnp.float32),
        lax.psum_scatter(
            grad_out_bias.astype(jnp.bfloat16), "grp", scatter_dimension=0, tiled=True
        ).astype(jnp.float32),
        lax.psum_scatter(
            grad_gain_one.astype(jnp.bfloat16), "grp", scatter_dimension=0, tiled=True
        ).astype(jnp.float32),
        lax.psum_scatter(
            grad_shift_one.astype(jnp.bfloat16), "grp", scatter_dimension=0, tiled=True
        ).astype(jnp.float32),
        lax.psum_scatter(
            grad_gain_two.astype(jnp.bfloat16), "grp", scatter_dimension=0, tiled=True
        ).astype(jnp.float32),
        lax.psum_scatter(
            grad_shift_two.astype(jnp.bfloat16), "grp", scatter_dimension=0, tiled=True
        ).astype(jnp.float32),
        lax.psum_scatter(
            grad_up_weight.astype(jnp.bfloat16), "grp", scatter_dimension=0, tiled=True
        ).astype(jnp.float32),
        lax.psum_scatter(
            grad_up_bias.astype(jnp.bfloat16), "grp", scatter_dimension=0, tiled=True
        ).astype(jnp.float32),
        lax.psum_scatter(
            grad_down_weight.astype(jnp.bfloat16), "grp", scatter_dimension=0, tiled=True
        ).astype(jnp.float32),
        lax.psum_scatter(
            grad_down_bias.astype(jnp.bfloat16), "grp", scatter_dimension=0, tiled=True
        ).astype(jnp.float32),
    )
    totals = (
        lax.psum(shares[0].astype(jnp.bfloat16), "rep").astype(jnp.float32),
        lax.psum(shares[1].astype(jnp.bfloat16), "rep").astype(jnp.float32),
        lax.psum(shares[2].astype(jnp.bfloat16), "rep").astype(jnp.float32),
        lax.psum(shares[3].astype(jnp.bfloat16), "rep").astype(jnp.float32),
        lax.psum(shares[4].astype(jnp.bfloat16), "rep").astype(jnp.float32),
        lax.psum(shares[5].astype(jnp.bfloat16), "rep").astype(jnp.float32),
        lax.psum(shares[6].astype(jnp.bfloat16), "rep").astype(jnp.float32),
        lax.psum(shares[7].astype(jnp.bfloat16), "rep").astype(jnp.float32),
        lax.psum(shares[8].astype(jnp.bfloat16), "rep").astype(jnp.float32),
        lax.psum(shares[9].astype(jnp.bfloat16), "rep").astype(jnp.float32),
        lax.psum(shares[10].astype(jnp.bfloat16), "rep").astype(jnp.float32),
        lax.psum(shares[11].astype(jnp.bfloat16), "rep").astype(jnp.float32),
        lax.psum(shares[12].astype(jnp.bfloat16), "rep").astype(jnp.float32),
        lax.psum(shares[13].astype(jnp.bfloat16), "rep").astype(jnp.float32),
        lax.psum(shares[14].astype(jnp.bfloat16), "rep").astype(jnp.float32),
    )
    return (
        layer_out,
        tokens_grad,
        totals[0],
        totals[1],
        totals[2],
        totals[3],
        totals[4],
        totals[5],
        totals[6],
        totals[7],
        totals[8],
        totals[9],
        totals[10],
        totals[11],
        totals[12],
        totals[13],
        totals[14],
    )


def solution(mesh):
    placed = (
        P("rep", "grp", None),
        P("grp", None),
        P("grp", None),
        P("grp", None),
        P("grp"),
        P("grp"),
        P("grp", None),
        P("grp"),
        P("grp"),
        P("grp"),
        P("grp"),
        P("grp"),
        P("grp", None),
        P("grp"),
        P("grp", None),
        P("grp"),
        P("rep", "grp", None),
    )
    return jax.shard_map(
        body,
        mesh=mesh,
        in_specs=placed,
        out_specs=(
            P("rep", "grp", None),
            P("rep", "grp", None),
            P("grp", None),
            P("grp", None),
            P("grp", None),
            P("grp"),
            P("grp"),
            P("grp", None),
            P("grp"),
            P("grp"),
            P("grp"),
            P("grp"),
            P("grp"),
            P("grp", None),
            P("grp"),
            P("grp", None),
            P("grp"),
        ),
        check_vma=False,
    )
```

profile of v0, /device:TPU:0, one launch (start us, length us, event | category | flops | bytes accessed | tf_op | source)
XLA Modules:
  0.0 1362.8 jit_solution(9006401191543345832)
XLA Ops:
  21.4 23.9 %all-gather.23.cloned.1.call-done = bf16[1024,1024]{1,0:T(8,128)(2,1)} async-done(((bf16[512,1024]{1,0:T(8,128)(2,1)}), bf16[1024,1024]{1,0:T(8,128)(2,1)}) %all-gather.23.cloned.1.call-update) | async-done | bytes 2097168 | tf_op jit(solution)/shard_map/all_gather | solution.py:132
  54.5 25.6 %all-gather.19.cloned.1.call-done = bf16[1024,1024]{1,0:T(8,128)(2,1)} async-done(((bf16[512,1024]{1,0:T(8,128)(2,1)}), bf16[1024,1024]{1,0:T(8,128)(2,1)}) %all-gather.19.cloned.1.call-update) | async-done | bytes 2097168 | tf_op jit(solution)/shard_map/all_gather | solution.py:133
  121.2 41.4 %all-gather.33.cloned.1.call-done = bf16[1568,1024]{1,0:T(8,128)(2,1)} async-done(((bf16[784,1024]{1,0:T(8,128)(2,1)}), bf16[1568,1024]{1,0:T(8,128)(2,1)}) %all-gather.33.cloned.1.call-update) | async-done | bytes 3211280 | tf_op jit(solution)/shard_map/all_gather | solution.py:189
  166.9 31.9 %multiply_reduce_fusion.1 = (f32[16,784]{1,0:T(8,128)S(1)}, f32[16,784,1568]{2,1,0:T(8,128)}) fusion(bf16[784,16,64]{0,2,1:T(8,128)(2,1)} %bitcast.148, bf16[1568,16,64]{0,2,1:T(8,128)(2,1)S(1)} %bitcast.144), kind=kOutput, calls=%fused_computation.6 | convolution fusion | flops 2556956416 | bytes 83543040 | tf_op jit(solution)/shard_map/while/body/eval_jaxpr/qhd,khd->hqk/dot_general | solution.py:55
  198.8 27.1 %fusion = f32[16,784]{1,0:T(8,128)S(1)} fusion(f32[16,784,1568]{2,1,0:T(8,128)} %get-tuple-element.101, f32[16,784]{1,0:T(8,128)S(1)} %get-tuple-element.100), kind=kLoop, calls=%fused_computation.5 | loop fusion | flops 58994432 | bytes 78776320 | tf_op jit(solution)/shard_map/while/body/eval_jaxpr/reduce_sum | solution.py:65
  231.9 36.9 %fusion.42 = bf16[16,64,784]{2,1,0:T(8,128)(2,1)} fusion(bf16[1568,16,64]{0,2,1:T(8,128)(2,1)} %bitcast.154, f32[16,784,1568]{2,1,0:T(8,128)} %get-tuple-element.101, f32[16,784]{1,0:T(8,128)S(1)} %fusion, f32[16,784]{1,0:T(8,128)S(1)} %get-tuple-element.100), kind=kOutput, calls=%fused_computation.84 | convolution fusion | flops 2597109760 | bytes 83593216 | tf_op jit(solution)/shard_map/while/body/eval_jaxpr/hqk,khd->qhd/dot_general | solution.py:67
  275.3 75.0 %all-gather.27.cloned.1.call-done = bf16[1024,4096]{1,0:T(8,128)(2,1)} async-done(((bf16[512,4096]{1,0:T(8,128)(2,1)}), bf16[1024,4096]{1,0:T(8,128)(2,1)}) %all-gather.27.cloned.1.call-update) | async-done | bytes 8388624 | tf_op jit(solution)/shard_map/all_gather | solution.py:158
  350.3 40.1 %multiply_convert_fusion.1 = (bf16[784,4096]{1,0:T(8,128)(2,1)}, f32[784,4096]{1,0:T(8,128)}, f32[784,4096]{1,0:T(8,128)}) fusion(f32[4096]{0:T(1024)S(1)} %copy-done.34, bf16[1024,4096]{1,0:T(8,128)(2,1)} %all-gather.27.cloned.1.call-done, f32[784,1024]{1,0:T(8,128)} %copy-done.7, f32[1024]{0:T(1024)S(1)} %bitcast.178, f32[1024]{0:T(1024)S(1)} %bitcast.168, ...), kind=kOutput, calls=%fused_computation.13 | convolution fusion | flops 6792626176 | bytes 43743360 | tf_op jit(solution)/shard_map/dot_general | solution.py:32
  390.4 65.5 %all-gather.29.cloned.1.call-done = bf16[4096,1024]{1,0:T(8,128)(2,1)} async-done(((bf16[2048,1024]{1,0:T(8,128)(2,1)}), bf16[4096,1024]{1,0:T(8,128)(2,1)}) %all-gather.29.cloned.1.call-update) | async-done | bytes 8388624 | tf_op jit(solution)/shard_map/all_gather | solution.py:162
  455.9 21.8 %fusion.65 = (bf16[4096]{0:T(1024)(128)(2,1)}, bf16[784,4096]{1,0:T(8,128)(2,1)}) fusion(f32[784,4096]{1,0:T(8,128)} %get-tuple-element.99, bf16[4096,1024]{1,0:T(8,128)(2,1)} %all-gather.29.cloned.1.call-done, bf16[1,784,1024]{2,1,0:T(8,128)(2,1)} %param.33, f32[784,4096]{1,0:T(8,128)} %get-tuple-element.104, f32[4096]{0:T(1024)S(1)} %copy-done.34), kind=kOutput, calls=%fused_computation.110 | convolution fusion | flops 6628044800 | bytes 42131456 | tf_op jit(solution)/shard_map/dot_general | solution.py:36
  477.7 12.7 multiply_reduce_fusion.2
  497.8 30.6 %fusion.19 = bf16[16,64,1568]{2,1,0:T(8,128)(2,1)} fusion(bf16[784,16,64]{0,2,1:T(8,128)(2,1)S(1)} %bitcast.150, f32[16,784,1568]{2,1,0:T(8,128)} %get-tuple-element.101, f32[16,784]{1,0:T(8,128)S(1)} %copy-done.11), kind=kOutput, calls=%fused_computation.41 | convolution fusion | flops 2578243584 | bytes 83543040 | tf_op jit(solution)/shard_map/while/body/eval_jaxpr/hqk,qhd->khd/dot_general | solution.py:91
  528.4 56.5 %multiply_reduce_fusion = (f32[16,784]{1,0:T(8,128)S(1)}, f32[16,784,1568]{2,1,0:T(8,128)}) fusion(f32[16,784,1568]{2,1,0:T(8,128)} %get-tuple-element.101, f32[16,784]{1,0:T(8,128)S(1)} %copy-done.11, bf16[784,16,64]{0,2,1:T(8,128)(2,1)S(1)} %bitcast.151, bf16[1568,16,64]{0,2,1:T(8,128)(2,1)} %bitcast.155), kind=kOutput, calls=%fused_computation.1 | convolution fusion | flops 2596294400 | bytes 162269184 | tf_op jit(solution)/shard_map/while/body/eval_jaxpr/qhd,khd->hqk/dot_general | solution.py:88
  584.9 16.1 %copy.52 = bf16[1,1568,1024]{2,0,1:T(2,128)(2,1)} copy(bf16[1,1568,1024]{1,2,0:T(8,128)(2,1)} %bitcast.152) | data formatting | bytes 6422528
  606.9 66.3 %multiply_convert_fusion = bf16[16,784,1568]{2,1,0:T(8,128)(2,1)} fusion(f32[16,784,1568]{2,1,0:T(8,128)} %get-tuple-element.107, f32[16,784,1568]{2,1,0:T(8,128)} %get-tuple-element.101, f32[16,784]{1,0:T(8,128)S(1)} %get-tuple-element.106, f32[16,784]{1,0:T(8,128)S(1)} %copy-done.11), kind=kLoop, calls=%fused_computation | loop fusion | flops 98344960 | bytes 196790272 | tf_op jit(solution)/shard_map/while/body/eval_jaxpr/convert_element_type | solution.py:93
  673.2 18.0 %multiply_convert_fusion.2 = bf16[16,64,1568]{2,1,0:T(8,128)(2,1)} fusion(bf16[784,16,64]{0,2,1:T(8,128)(2,1)S(1)} %bitcast.149, bf16[16,784,1568]{2,1,0:T(8,128)(2,1)} %multiply_convert_fusion), kind=kOutput, calls=%fused_computation.29 | convolution fusion | flops 2520842240 | bytes 44154880 | tf_op jit(solution)/shard_map/while/body/eval_jaxpr/hqk,qhd->khd/dot_general | solution.py:99
  691.3 16.1 %copy.50 = bf16[1,1568,1024]{2,0,1:T(2,128)(2,1)} copy(bf16[1,1568,1024]{1,2,0:T(8,128)(2,1)} %bitcast.153) | data formatting | bytes 6422528
  719.6 21.1 %bitcast_reduce_fusion = (bf16[16,64]{1,0:T(8,128)(2,1)S(1)}, bf16[16,64,784]{2,1,0:T(8,128)(2,1)}) fusion(bf16[1568,16,64]{0,2,1:T(8,128)(2,1)S(1)} %bitcast.145, bf16[16,784,1568]{2,1,0:T(8,128)(2,1)} %multiply_convert_fusion), kind=kOutput, calls=%fused_computation.83 | convolution fusion | flops 2520038400 | bytes 44156928 | tf_op jit(solution)/shard_map/while/body/eval_jaxpr/hqk,khd->qhd/dot_general | solution.py:95
  747.0 7.5 fusion.62
  754.5 8.2 copy.53
  771.7 7.9 copy.51
  783.8 14.6 %convolution_convert_fusion = bf16[1024,4096]{1,0:T(8,128)(2,1)} fusion(bf16[784,4096]{1,0:T(8,128)(2,1)} %get-tuple-element.112, f32[784,1024]{1,0:T(8,128)} %copy-done.7, f32[1024]{0:T(1024)S(1)} %bitcast.179, f32[1024]{0:T(1024)S(1)} %bitcast.171, f32[784]{0:T(1024)S(1)} %copy-done.33, f32[784]{0:T(1024)S(1)} %copy-done.25), kind=kOutput, calls=%fused_computation.27 | convolution fusion | flops 6584877056 | bytes 18036864 | tf_op jit(solution)/shard_map/dot_general | solution.py:42
  799.9 14.9 %convolution_convert_fusion.1 = bf16[4096,1024]{1,0:T(8,128)(2,1)} fusion(bf16[784,4096]{1,0:T(8,128)(2,1)} %get-tuple-element.98, bf16[1,784,1024]{2,1,0:T(8,128)(2,1)S(1)} %copy-done.10), kind=kOutput, calls=%fused_computation.28 | convolution fusion | flops 6580862976 | bytes 16416768 | tf_op jit(solution)/shard_map/dot_general | solution.py:42
  814.9 12.0 reduce-scatter.13.cloned.1.call-done
  826.9 34.8 %reduce-scatter.17.cloned.1.call-done = bf16[512,1024]{1,0:T(8,128)(2,1)} async-done(((bf16[1024,1024]{1,0:T(8,128)(2,1)}), bf16[512,1024]{1,0:T(8,128)(2,1)}) %reduce-scatter.17.cloned.1.call-update) | async-done | bytes 1048592 | tf_op jit(solution)/shard_map/reduce_scatter | solution.py:303
  861.7 34.6 %reduce-scatter.15.cloned.1.call-done = bf16[512,1024]{1,0:T(8,128)(2,1)} async-done(((bf16[1024,1024]{1,0:T(8,128)(2,1)}), bf16[512,1024]{1,0:T(8,128)(2,1)}) %reduce-scatter.15.cloned.1.call-update) | async-done | bytes 1048592 | tf_op jit(solution)/shard_map/reduce_scatter | solution.py:300
  896.3 102.1 %reduce-scatter.21.cloned.1.call-done = bf16[512,4096]{1,0:T(8,128)(2,1)} async-done(((bf16[1024,4096]{1,0:T(8,128)(2,1)}), bf16[512,4096]{1,0:T(8,128)(2,1)}) %reduce-scatter.21.cloned.1.call-update) | async-done | bytes 4194320 | tf_op jit(solution)/shard_map/reduce_scatter | solution.py:330
  998.4 102.1 %reduce-scatter.23.cloned.1.call-done = bf16[2048,1024]{1,0:T(8,128)(2,1)} async-done(((bf16[4096,1024]{1,0:T(8,128)(2,1)}), bf16[2048,1024]{1,0:T(8,128)(2,1)}) %reduce-scatter.23.cloned.1.call-update) | async-done | bytes 4194320 | tf_op jit(solution)/shard_map/reduce_scatter | solution.py:336
  1107.8 13.4 fusion.43
  1130.6 6.9 all-reduce.11
  1138.0 61.5 %all-reduce.9 = (bf16[512]{0:T(512)(128)(2,1)S(1)}, bf16[512]{0:T(512)(128)(2,1)S(1)}, bf16[512]{0:T(512)(128)(2,1)S(1)}, bf16[512]{0:T(512)(128)(2,1)S(1)}, bf1...) all-reduce(bf16[512]{0:T(512)(128)(2,1)S(1)} %dynamic-slice.4, ...), channel_id=1, replica_groups=mesh['rep'=16,'grp'=2] {'rep'}, use_global_device_ids=true, to_apply=%region_21.22 | all-reduce | flops 6144 | bytes 24576 | tf_op jit(solution)/shard_map/psum | solution.py:347
  1209.2 130.1 %all-reduce.14.cloned.1.call-done = (bf16[512,1024]{1,0:T(8,128)(2,1)}, bf16[512,1024]{1,0:T(8,128)(2,1)}, bf16[512,1024]{1,0:T(8,128)(2,1)}, bf16[512,1024]{1,0...) async-done(((bf16[512,1024]{1,0:T(8,128)(2,1)}, bf16[512,1024]{1,0:T(8,128)(2,1)}, bf16[512,1024]{1,0:T(8,128)(2,1)}, bf16[512,1024]{1,0:T(8,128)(2,1)}, ...) | async-done | bytes 12582928 | tf_op jit(solution)/shard_map/psum | solution.py:344
  (246 shorter events, 169.1 us)
Async XLA Ops:
  7.2 38.2 %all-gather.23.cloned.1.call-start = ((), (), s32[]{:S(2)}) async-start(), calls=%async_computation.10 | async-start | bytes 3145728 | tf_op jit(solution)/shard_map/all_gather | solution.py:132
  7.9 72.1 %all-gather.19.cloned.1.call-start = ((), (), s32[]{:S(2)}) async-start(), calls=%async_computation.8 | async-start | bytes 3145728 | tf_op jit(solution)/shard_map/all_gather | solution.py:133
  8.7 106.3 %all-gather.21.cloned.1.call-start = ((), (), s32[]{:S(2)}) async-start(), calls=%async_computation.9 | async-start | bytes 3145728 | tf_op jit(solution)/shard_map/all_gather | solution.py:131
  9.4 153.2 %all-gather.33.cloned.1.call-start = ((), (), s32[]{:S(2)}) async-start(), calls=%async_computation.21 | async-start | bytes 4816896 | tf_op jit(solution)/shard_map/all_gather | solution.py:189
  16.1 98.8 %copy-start.38 = (f32[2,1,512]{2,1,0:T(1,128)}, f32[2,1,512]{2,1,0:T(1,128)S(1)}, u32[]{:S(2)}) copy-start(f32[2,1,512]{2,1,0:T(1,128)S(1)} %convert_element_type.380) | copy-start | bytes 12292
  20.5 94.4 %copy-start.26 = (f32[2,1,512]{2,1,0:T(1,128)}, f32[2,1,512]{2,1,0:T(1,128)S(1)}, u32[]{:S(2)}) copy-start(f32[2,1,512]{2,1,0:T(1,128)S(1)} %convert_element_type.379) | copy-start | bytes 12292
  20.8 94.1 %copy-start.22 = (f32[784]{0:T(1024)}, f32[784]{0:T(1024)S(1)}, u32[]{:S(2)}) copy-start(f32[784]{0:T(1024)S(1)} %broadcast_multiply_fusion.5) | copy-start | bytes 9412
  21.4 93.5 %copy-start.28 = (f32[784]{0:T(1024)}, f32[784]{0:T(1024)S(1)}, u32[]{:S(2)}) copy-start(f32[784]{0:T(1024)S(1)} %add_rsqrt_fusion.1) | copy-start | bytes 9412
  50.1 176.5 %all-gather.31.cloned.1.call-start = ((), (), s32[]{:S(2)}) async-start(), calls=%async_computation.20 | async-start | bytes 4816896 | tf_op jit(solution)/shard_map/all_gather | solution.py:190
  84.7 184.1 %all-gather.25.cloned.1.call-start = ((), (), s32[]{:S(2)}) async-start(), calls=%async_computation.11 | async-start | bytes 3145728 | tf_op jit(solution)/shard_map/all_gather | solution.py:140
  85.3 21.4 %copy-start.36 = (f32[2048]{0:T(1024)S(1)}, f32[2048]{0:T(1024)}, u32[]{:S(2)}) copy-start(f32[2048]{0:T(1024)} %param.30) | copy-start | bytes 24580
  85.4 265.0 %all-gather.27.cloned.1.call-start = ((), (), s32[]{:S(2)}) async-start(), calls=%async_computation.12 | async-start | bytes 12582912 | tf_op jit(solution)/shard_map/all_gather | solution.py:158
  86.1 369.8 %all-gather.29.cloned.1.call-start = ((), (), s32[]{:S(2)}) async-start(), calls=%async_computation.13 | async-start | bytes 12582912 | tf_op jit(solution)/shard_map/all_gather | solution.py:162
  86.8 660.1 %reduce-scatter.27.cloned.1.call-start = ((), (), s32[]{:S(2)}) async-start(), calls=%async_computation.23 | async-start | bytes 4816896
  166.9 31.9 %copy-start = (bf16[1568,1024]{0,1:T(8,128)(2,1)}, bf16[1568,1024]{0,1:T(8,128)(2,1)S(1)}, u32[]{:S(2)}) copy-start(bf16[1568,1024]{0,1:T(8,128)(2,1)S(1)} %copy.48) | copy-start | bytes 9633796
  231.9 36.9 %copy-start.4 = (bf16[1,784,1024]{2,1,0:T(8,128)(2,1)S(1)}, bf16[1,784,1024]{2,1,0:T(8,128)(2,1)}, u32[]{:S(2)}) copy-start(bf16[1,784,1024]{2,1,0:T(8,128)(2,1)} %param.17) | copy-start | bytes 4816900
  231.9 36.9 %copy-start.42 = (f32[2,1,512]{2,1,0:T(1,128)S(1)}, f32[2,1,512]{2,1,0:T(1,128)}, u32[]{:S(2)}) copy-start(f32[2,1,512]{2,1,0:T(1,128)} %convert_element_type.383) | copy-start | bytes 12292
  273.1 77.2 %copy-start.30 = (f32[2,1,512]{2,1,0:T(1,128)S(1)}, f32[2,1,512]{2,1,0:T(1,128)}, u32[]{:S(2)}) copy-start(f32[2,1,512]{2,1,0:T(1,128)} %convert_element_type.384) | copy-start | bytes 12292
  273.2 77.2 %copy-start.34 = (f32[4096]{0:T(1024)S(1)}, f32[4096]{0:T(1024)}, u32[]{:S(2)}) copy-start(f32[4096]{0:T(1024)} %convert_element_type.329) | copy-start | bytes 49156
  273.2 77.2 %copy-start.40 = (f32[2,1,512]{2,1,0:T(1,128)S(1)}, f32[2,1,512]{2,1,0:T(1,128)}, u32[]{:S(2)}) copy-start(f32[2,1,512]{2,1,0:T(1,128)} %convert_element_type.385) | copy-start | bytes 12292
  273.2 217.2 %copy-start.24 = (f32[784]{0:T(1024)}, f32[784]{0:T(1024)S(1)}, u32[]{:S(2)}) copy-start(f32[784]{0:T(1024)S(1)} %broadcast_multiply_fusion.4) | copy-start | bytes 9412
  275.3 215.1 %copy-start.32 = (f32[784]{0:T(1024)}, f32[784]{0:T(1024)S(1)}, u32[]{:S(2)}) copy-start(f32[784]{0:T(1024)S(1)} %add_rsqrt_fusion) | copy-start | bytes 9412
  455.9 21.8 %copy-start.8 = (f32[784,1024]{1,0:T(8,128)S(1)}, f32[784,1024]{1,0:T(8,128)}, u32[]{:S(2)}) copy-start(f32[784,1024]{1,0:T(8,128)} %copy-done.7) | copy-start | bytes 9633796
  606.9 160.0 %reduce-scatter.25.cloned.1.call-start = ((), (), s32[]{:S(2)}) async-start(), calls=%async_computation.22 | async-start | bytes 4816896
  606.9 66.3 %copy-start.2 = (bf16[784,1024]{0,1:T(8,128)(2,1)S(1)}, bf16[784,1024]{0,1:T(8,128)(2,1)}, u32[]{:S(2)}) copy-start(bf16[784,1024]{0,1:T(8,128)(2,1)} %copy.47) | copy-start | bytes 4816900
  713.2 101.7 %reduce-scatter.19.cloned.1.call-start = ((), (), s32[]{:S(2)}) async-start(), calls=%async_computation.17 | async-start | bytes 3145728 | tf_op jit(solution)/shard_map/reduce_scatter | solution.py:312
  719.6 107.3 %reduce-scatter.13.cloned.1.call-start = ((), (), s32[]{:S(2)}) async-start(), calls=%async_computation.14 | async-start | bytes 3145728 | tf_op jit(solution)/shard_map/reduce_scatter | solution.py:297
  746.9 114.8 %reduce-scatter.17.cloned.1.call-start = ((), (), s32[]{:S(2)}) async-start(), calls=%async_computation.16 | async-start | bytes 3145728 | tf_op jit(solution)/shard_map/reduce_scatter | solution.py:303
  766.8 129.5 %reduce-scatter.15.cloned.1.call-start = ((), (), s32[]{:S(2)}) async-start(), calls=%async_computation.15 | async-start | bytes 3145728 | tf_op jit(solution)/shard_map/reduce_scatter | solution.py:300
  783.7 214.6 %reduce-scatter.21.cloned.1.call-start = ((), (), s32[]{:S(2)}) async-start(), calls=%async_computation.18 | async-start | bytes 12582912 | tf_op jit(solution)/shard_map/reduce_scatter | solution.py:330
  798.5 302.0 %reduce-scatter.23.cloned.1.call-start = ((), (), s32[]{:S(2)}) async-start(), calls=%async_computation.19 | async-start | bytes 12582912 | tf_op jit(solution)/shard_map/reduce_scatter | solution.py:336
  814.9 524.4 %all-reduce.14.cloned.1.call-start = ((), (), s32[]{:S(2)}) async-start(), calls=%async_computation.24 | async-start | bytes 25165824 | tf_op jit(solution)/shard_map/psum | solution.py:344
  (41 other events, 249.2 us)
Sparse Core Ops, SparseCore 0:
  9.6 35.8 all-gather.22
  46.9 33.0 all-gather.18
  81.6 33.2 all-gather.20
  116.9 45.6 all-gather.32
  164.6 45.6 all-gather.30
  211.7 33.0 all-gather.24
  246.3 103.9 all-gather.26
  351.9 103.9 all-gather.28
  607.0 44.1 reduce-scatter.26
  713.3 44.2 reduce-scatter.24
  760.4 31.8 reduce-scatter.18
  795.0 31.8 reduce-scatter.12
  829.7 31.8 reduce-scatter.16
  864.3 31.8 reduce-scatter.14
  899.0 99.3 reduce-scatter.20
  1001.1 99.3 reduce-scatter.22
  1105.4 233.7 all-reduce.13
where the time goes:
time: 1370 us; the launch traced here: 1360 us
  waiting for transfers between devices  654 us (48%)
  matrix products  361 us (26%)
  other arithmetic  135 us (10%)
  blocking collectives  109 us (8%)
  local copies, waits for them, and re-layouts  85.8 us (6%)
  between operations  16.2 us (1%)
    psum x1, waiting for transfers between devices, body(): lax.psum(shares[0].astype(jnp.bfloat16), 'rep').astype(jnp.float32)  130 us
    reduce_scatter x1, waiting for transfers between devices, body(): lax.psum_scatter(grad_down_weight.astype(jnp.bfloat16), 'grp', scatter_di...  102 us
    reduce_scatter x1, waiting for transfers between devices, body(): lax.psum_scatter(grad_up_weight.astype(jnp.bfloat16), 'grp', scatter_dime...  102 us
    all_gather x1, waiting for transfers between devices, body(): lax.all_gather(up_weight, 'grp', axis=0, tiled=True)  75 us
    unnamed x137, local copies, waits for them, and re-layouts  71.7 us
    dot_general x6, matrix products, matmul(): return jnp.dot(left, right, preferred_element_type=jnp.float32)  70.5 us
    convert_element_type x1, other arithmetic, attend_back(): grad_scores = (weights * (grad_probs - inner)).astype(jnp.bfloat16)  66.3 us
    all_gather x1, waiting for transfers between devices, body(): lax.all_gather(down_weight, 'grp', axis=0, tiled=True)  65.5 us
  transfers between devices with their start and end apart: 17, of which 12 were waited for; matrix products, arithmetic and copies ran while one was open for 30% of the time, Pallas kernels for 0%

commit v1 on v0

--- a/solution.py
+++ b/solution.py
@@ -106,7 +106,7 @@
     )
 
 
-def body(
+def spread_body(
     tokens,
     query_weight,
     key_weight,
@@ -378,7 +378,258 @@
     )
 
 
+def flip(values, axis, size, bit):
+    mask = 1 << bit
+    return lax.ppermute(values, axis, [(at, at ^ mask) for at in range(size)])
+
+
+def ordered(mine, theirs, place, axis=0):
+    first = jnp.where(place == 0, mine, theirs)
+    last = jnp.where(place == 0, theirs, mine)
+    return jnp.concatenate((first, last), axis=axis)
+
+
+def pick_part(values, place):
+    rows, width = values.shape
+    blocks = values.reshape(rows, 2, 2, width // 4)
+    return lax.dynamic_index_in_dim(blocks, place, axis=2, keepdims=False).reshape(
+        rows, width // 2
+    )
+
+
+def join_parts(mine, theirs, place):
+    rows, width = mine.shape
+    mine = mine.reshape(rows, 2, 1, width // 2)
+    theirs = theirs.reshape(rows, 2, 1, width // 2)
+    return ordered(mine, theirs, place, axis=2).reshape(rows, 2 * width)
+
+
+def paired_body(
+    rep_size,
+    tokens,
+    query_weight,
+    key_weight,
+    value_weight,
+    query_bias,
+    value_bias,
+    out_weight,
+    out_bias,
+    first_gain,
+    first_shift,
+    second_gain,
+    second_shift,
+    up_weight,
+    up_bias,
+    down_weight,
+    down_bias,
+    cotangent,
+):
+    low = jnp.bfloat16
+    wide = jnp.float32
+    rep_bits = rep_size.bit_length() - 1
+    rep_at = lax.axis_index("rep")
+    grp_at = lax.axis_index("grp")
+    core_at = rep_at & 1
+    length, width = tokens.shape[1], tokens.shape[2]
+    shard = width // 2
+    devices = [(rep, grp) for rep in range(rep_size) for grp in range(2)]
+    swap = [
+        (2 * rep + grp, 2 * (rep - rep % 2 + grp) + rep % 2)
+        for rep, grp in devices
+        if rep % 2 != grp
+    ]
+
+    def swap_clips(values):
+        moved = lax.ppermute(values, ("rep", "grp"), swap)
+        return jnp.where(core_at == grp_at, values, moved)
+
+    def over_core(values):
+        return flip(values, "rep", rep_size, 0)
+
+    def over_group(values):
+        return flip(values, "grp", 2, 0)
+
+    vectors = (
+        query_bias,
+        value_bias,
+        out_bias,
+        first_gain,
+        first_shift,
+        second_gain,
+        second_shift,
+        up_bias,
+        down_bias,
+    )
+    packed = jnp.concatenate(vectors).reshape(-1, 128)
+    packed_two = ordered(packed[None], over_group(packed)[None], grp_at).reshape(2, -1)
+    whole, start = [], 0
+    for vector in vectors:
+        whole.append(packed_two[:, start : start + vector.shape[0]].reshape(-1))
+        start += vector.shape[0]
+    qbias, vbias, obias, gain_one, shift_one, gain_two, shift_two, ubias, dbias = whole
+
+    own_qkv = jnp.concatenate(
+        [pick_part(item, core_at) for item in (query_weight, key_weight, value_weight)], axis=1
+    )
+    if rep_bits > 1:
+        half = shard // 2
+        row_at = (rep_at >> 1) & 1
+        piece = over_group(lax.dynamic_slice_in_dim(own_qkv, row_at * half, half, 0))
+        other_qkv = ordered(piece, flip(piece, "rep", rep_size, 1), row_at)
+    else:
+        other_qkv = over_group(own_qkv)
+    tokens_own = swap_clips(tokens[0])
+    full_qkv = ordered(own_qkv, other_qkv, grp_at)
+    bias_qkv = jnp.concatenate(
+        (
+            pick_part(qbias[None], core_at)[0],
+            jnp.zeros((shard,), wide),
+            pick_part(vbias[None], core_at)[0],
+        )
+    )
+    grad_own = swap_clips(cotangent[0])
+
+    def gather_weight(weight, after):
+        rows = weight.shape[0] // rep_size
+        piece = lax.dynamic_slice_in_dim(weight, rep_at * rows, rows, 0)
+        piece, _ = lax.optimization_barrier((piece, after))
+        return lax.all_gather(piece, ("grp", "rep"), axis=0, tiled=True)
+
+    full_out = gather_weight(out_weight, tokens_own)
+    full_up = gather_weight(up_weight, tokens_own)
+    full_down = gather_weight(down_weight, tokens_own)
+
+    inputs = tokens_own.astype(wide)
+    first_norm, first_normed, first_inverse = norm_parts(inputs, gain_one, shift_one)
+    first_low = first_norm.astype(low)
+    first_all = jnp.concatenate((first_low, over_core(first_low)), axis=0)
+    qkv = (matmul(first_all, full_qkv) + bias_qkv).astype(low)
+    queries, keys, values = qkv[:, :shard], qkv[:, shard : 2 * shard], qkv[:, 2 * shard :]
+    mixed_heads, log_total = attend_clip((queries, keys, values))
+    mixed_heads = mixed_heads.astype(low)
+    mixed_low = join_parts(mixed_heads[:length], over_core(mixed_heads[length:]), core_at)
+    middle = inputs + matmul(mixed_low, full_out) + obias
+    second_norm, second_normed, second_inverse = norm_parts(middle, gain_two, shift_two)
+    second_low = second_norm.astype(low)
+    hidden_pre = matmul(second_low, full_up) + ubias
+    hidden_low = jax.nn.gelu(hidden_pre, approximate=False).astype(low)
+    result = middle + matmul(hidden_low, full_down) + dbias
+    layer_out = swap_clips(result.astype(low))[None]
+
+    def both(values):
+        return jnp.concatenate((values, over_core(values)), axis=0)
+
+    def both_parts(values):
+        mine = pick_part(values, core_at)
+        return jnp.concatenate((mine, over_core(pick_part(values, 1 - core_at))), axis=0)
+
+    def column_half(values, place):
+        half = values.shape[1] // 2
+        return lax.dynamic_slice_in_dim(values, place * half, half, 1)
+
+    def add_up(left, right):
+        give = matmul_left_t(column_half(left, 1 - grp_at), right).astype(low)
+        part = matmul_left_t(column_half(left, grp_at), right) + over_group(give).astype(wide)
+        for bit in range(1, rep_bits):
+            half = part.shape[0] // 2
+            at = (rep_at >> bit) & 1
+            give = lax.dynamic_slice_in_dim(part, (1 - at) * half, half, 0).astype(low)
+            keep = lax.dynamic_slice_in_dim(part, at * half, half, 0)
+            part = keep + flip(give, "rep", rep_size, bit).astype(wide)
+        total = part.astype(low)
+        for bit in reversed(range(1, rep_bits)):
+            total = ordered(total, flip(total, "rep", rep_size, bit), (rep_at >> bit) & 1)
+        return total, over_core(total)
+
+    grad_wide = grad_own.astype(wide)
+    grad_all = both(grad_own)
+    down_total = add_up(both_parts(hidden_low), grad_all)
+    grad_hidden = matmul_right_t(grad_own, full_down)
+    unused_value, gelu_pull = jax.vjp(partial(jax.nn.gelu, approximate=False), hidden_pre)
+    grad_pre_low = gelu_pull(grad_hidden)[0].astype(low)
+    up_total = add_up(both(second_low), both_parts(grad_pre_low))
+    grad_second, grad_gain_two, grad_shift_two = norm_back(
+        matmul_right_t(grad_pre_low, full_up), second_normed, second_inverse, gain_two
+    )
+    grad_middle = grad_wide + grad_second
+    grad_middle_low = grad_middle.astype(low)
+    out_total = add_up(mixed_heads, both(grad_middle_low))
+    early = (
+        jnp.sum(grad_middle_low.astype(wide), axis=0),
+        grad_gain_two,
+        grad_shift_two,
+        jnp.sum(grad_pre_low.astype(wide), axis=0),
+        jnp.sum(grad_wide, axis=0),
+    )
+    grad_mixed_low = matmul_right_t(grad_middle_low, full_out).astype(low)
+    grad_mixed_heads = both_parts(grad_mixed_low)
+    grad_queries, grad_keys, grad_values = attend_back(
+        (queries, keys, values, grad_mixed_heads, log_total)
+    )
+    grad_qkv = jnp.concatenate((grad_queries, grad_keys, grad_values), axis=1).astype(low)
+    qkv_total = add_up(first_all, grad_qkv)
+    partial_first = matmul_right_t(grad_qkv[length:], full_qkv).astype(low)
+    grad_first_norm = matmul_right_t(grad_qkv[:length], full_qkv) + over_core(
+        partial_first
+    ).astype(wide)
+    grad_first, grad_gain_one, grad_shift_one = norm_back(
+        grad_first_norm, first_normed, first_inverse, gain_one
+    )
+    tokens_grad = swap_clips((grad_middle + grad_first).astype(low))[None]
+
+    head_bias = jnp.sum(grad_qkv.astype(wide), axis=0)
+    nothing = jnp.zeros((1, shard), wide)
+    late = (
+        join_parts(head_bias[None, :shard], nothing, core_at)[0],
+        join_parts(head_bias[None, 2 * shard :], nothing, core_at)[0],
+        grad_gain_one,
+        grad_shift_one,
+    )
+
+    def sum_vectors(items):
+        total = lax.psum(jnp.concatenate(items), ("rep", "grp"))
+        out, start = [], 0
+        for item in items:
+            size = item.shape[0] // 2
+            out.append(lax.dynamic_slice_in_dim(total, start + grp_at * size, size, 0))
+            start += 2 * size
+        return out
+
+    obias_grad, gain_two_grad, shift_two_grad, ubias_grad, dbias_grad = sum_vectors(early)
+    qbias_grad, vbias_grad, gain_one_grad, shift_one_grad = sum_vectors(late)
+
+    def wide_rows(pair):
+        return ordered(pair[0], pair[1], core_at).astype(wide)
+
+    def wide_columns(mine, theirs):
+        return join_parts(mine, theirs, core_at).astype(wide)
+
+    qkv_mine, qkv_theirs = qkv_total
+    return (
+        layer_out,
+        tokens_grad,
+        wide_columns(qkv_mine[:, :shard], qkv_theirs[:, :shard]),
+        wide_columns(qkv_mine[:, shard : 2 * shard], qkv_theirs[:, shard : 2 * shard]),
+        wide_columns(qkv_mine[:, 2 * shard :], qkv_theirs[:, 2 * shard :]),
+        qbias_grad,
+        vbias_grad,
+        wide_rows(out_total),
+        obias_grad,
+        gain_one_grad,
+        shift_one_grad,
+        gain_two_grad,
+        shift_two_grad,
+        wide_columns(*up_total),
+        ubias_grad,
+        wide_rows(down_total),
+        dbias_grad,
+    )
+
+
 def solution(mesh):
+    rep_size = mesh.shape["rep"]
+    paired = mesh.shape["grp"] == 2 and rep_size > 1 and rep_size & (rep_size - 1) == 0
+    body = partial(paired_body, rep_size) if paired else spread_body
     placed = (
         P("rep", "grp", None),
         P("grp", None),

time: 1370 us -> 1310 us (0.956)
  waiting for transfers between devices: 654 us -> 269 us
  local copies, waits for them, and re-layouts: 85.8 us -> 412 us
  blocking collectives: 109 us -> 38.8 us
  starting transfers between devices: 0.69 us -> 68.7 us
  matrix products: 361 us -> 327 us
  other arithmetic: 135 us -> 167 us
    reduce_scatter x6 -> x0, waiting for transfers between devices: 286 us -> none  [the longest x1 102 us: body(): lax.psum_scatter(grad_down_weight.astype(jnp.bfloat16), 'grp', scatter_di...]
    ppermute x0 -> x48, waiting for transfers between devices: none -> 269 us  [the longest x44 269 us: flip(): return lax.ppermute(values, axis, [(at, at ^ mask) for at in range(size)])]
    dynamic_slice x0 -> x16, local copies, waits for them, and re-layouts: none -> 248 us  [the longest x9 242 us: pick_part(): lax.dynamic_index_in_dim(blocks, place, axis=2, keepdims=False)]
    all_gather x8 -> x3, waiting for transfers between devices: 234 us -> 0.01 us  [gather_weight(): return lax.all_gather(piece, ('grp', 'rep'), axis=0, tiled=True)]
    psum x1 -> x0, waiting for transfers between devices: 130 us -> none  [body(): lax.psum(shares[0].astype(jnp.bfloat16), 'rep').astype(jnp.float32)]
    ppermute x0 -> x48, starting transfers between devices: none -> 68.6 us  [the longest x44 61.7 us: flip(): return lax.ppermute(values, axis, [(at, at ^ mask) for at in range(size)])]
    reshape x0 -> x7, local copies, waits for them, and re-layouts: none -> 47 us  [the longest x6 42.1 us: pick_part(): blocks = values.reshape(rows, 2, 2, width // 4)]
    all_gather x9 -> x0, blocking collectives: 40.9 us -> none  [the longest x1 5.28 us: body(): lax.all_gather(first_shift.astype(jnp.bfloat16), 'grp', axis=0, tiled=True)]
  transfers between devices with their start and end apart: 17 -> 51, of which waited for: 12 -> 19; matrix products, arithmetic and copies ran while one was open for 30% -> 69% of each run, Pallas kernels for 0% -> 0%
where the time goes in v1:
time: 1310 us; the launch traced here: 1300 us
  local copies, waits for them, and re-layouts  412 us (31%)
  matrix products  327 us (25%)
  waiting for transfers between devices  269 us (21%)
  other arithmetic  167 us (13%)
  starting transfers between devices  68.7 us (5%)
  blocking collectives  38.8 us (3%)
  between operations  15.8 us (1%)
    ppermute x44, waiting for transfers between devices, flip(): return lax.ppermute(values, axis, [(at, at ^ mask) for at in range(size)])  269 us
    dynamic_slice x9, local copies, waits for them, and re-layouts, pick_part(): lax.dynamic_index_in_dim(blocks, place, axis=2, keepdims=False)  242 us
    convert_element_type x1, other arithmetic, attend_back(): grad_scores = (weights * (grad_probs - inner)).astype(jnp.bfloat16)  64.9 us
    dot_general x5, matrix products, matmul_right_t(): lax.dot_general(left, right, (((1,), (1,)), ((), ())), preferred_element_...  62.5 us
    ppermute x44, starting transfers between devices, flip(): return lax.ppermute(values, axis, [(at, at ^ mask) for at in range(size)])  61.7 us
    dot_general x1, matrix products, attend_back(): jnp.einsum('qhd,khd->hqk', grad_heads, split_heads(values), preferred_ele...  58.2 us
    reshape x6, local copies, waits for them, and re-layouts, pick_part(): blocks = values.reshape(rows, 2, 2, width // 4)  42.1 us
    psum x1, blocking collectives, sum_vectors(): total = lax.psum(jnp.concatenate(items), ('rep', 'grp'))  38.8 us
  transfers between devices with their start and end apart: 51, of which 19 were waited for; matrix products, arithmetic and copies ran while one was open for 69% of the time, Pallas kernels for 0%

profile of v1, /device:TPU:0, one launch (start us, length us, event | category | flops | bytes accessed | tf_op | source)
XLA Modules:
  0.0 1298.1 jit_solution(4979283539037769373)
XLA Ops:
  34.3 23.5 %collective-permute-start.3 = (bf16[256,1536]{1,0:T(8,128)(2,1)S(1)}, bf16[256,1536]{1,0:T(8,128)(2,1)S(1)}, u32[]{:S(2)}, u32[]{:S(2)}) collective-permute-start(bf16[256,1536]{1,0:T(8,128)(2,1)S(1)} %constant_dynamic-slice_fusion.6), channel_id=1, source_target_pairs={{0,1},{1,0},{2,3},{3,2},{4,5},{5,4},{6,7},{7,6},{8,9},{9,8},{10,11... | collective-permute-start | bytes 2359304 | tf_op jit(solution)/shard_map/ppermute | solution.py:383
  58.1 19.9 %collective-permute-done.1 = f32[48,128]{1,0:T(8,128)S(1)} collective-permute-done((f32[48,128]{1,0:T(8,128)S(1)}, f32[48,128]{1,0:T(8,128)S(1)}, u32[]{:S(2)}, u32[]{:S(2)}) %collective-permute-start.1) | collective-permute-done | bytes 24608 | tf_op jit(solution)/shard_map/ppermute | solution.py:383
  86.4 14.0 %collective-permute-done.4 = bf16[256,1536]{1,0:T(8,128)(2,1)} collective-permute-done((bf16[256,1536]{1,0:T(8,128)(2,1)S(1)}, bf16[256,1536]{1,0:T(8,128)(2,1)}, u32[]{:S(2)}, u32[]{:S(2)}) %collective-permute-start.4) | collective-permute-done | bytes 786464 | tf_op jit(solution)/shard_map/ppermute | solution.py:383
  121.2 31.3 %multiply_reduce_fusion.1 = (f32[8,1568]{1,0:T(8,128)S(1)}, f32[8,1568,1568]{1,2,0:T(8,128)}) fusion(bf16[1568,8,64]{0,2,1:T(8,128)(2,1)} %bitcast.125, bf16[1568,8,64]{0,2,1:T(8,128)(2,1)S(1)} %bitcast.123), kind=kOutput, calls=%fused_computation.6 | convolution fusion | flops 2556956416 | bytes 81937408 | tf_op jit(solution)/shard_map/qhd,khd->hqk/dot_general | solution.py:55
  152.5 26.7 %fusion = f32[8,1568]{1,0:T(8,128)S(1)} fusion(f32[8,1568,1568]{1,2,0:T(8,128)} %get-tuple-element.134, f32[8,1568]{1,0:T(8,128)S(1)} %get-tuple-element.133), kind=kLoop, calls=%fused_computation.5 | loop fusion | flops 58994432 | bytes 78776320 | tf_op jit(solution)/shard_map/reduce_sum | solution.py:65
  182.0 31.8 %fusion.34 = bf16[8,64,1568]{2,1,0:T(8,128)(2,1)} fusion(bf16[1568,8,64]{0,2,1:T(8,128)(2,1)S(1)} %bitcast.145, f32[8,1568,1568]{1,2,0:T(8,128)} %get-tuple-element.134, f32[8,1568]{1,0:T(8,128)S(1)} %fusion, f32[8,1568]{1,0:T(8,128)S(1)} %get-tuple-element.133), kind=kOutput, calls=%fused_computation.90 | convolution fusion | flops 2597109760 | bytes 81987584 | tf_op jit(solution)/shard_map/hqk,khd->qhd/dot_general | solution.py:67
  241.6 13.9 %fusion.97 = f32[784,4096]{1,0:T(8,128)} fusion(bf16[784,1024]{1,0:T(8,128)(2,1)} %add_convert_fusion.3, bf16[1024,4096]{1,0:T(8,128)(2,1)} %all-gather.6.cloned.1.call-done), kind=kOutput, calls=%fused_computation.298 | convolution fusion | flops 6576668672 | bytes 22839296 | tf_op jit(solution)/shard_map/dot_general | solution.py:32
  255.5 39.6 %convert_reduce_fusion = (f32[4096]{0:T(1024)S(1)}, bf16[784,4096]{1,0:T(8,128)(2,1)}, f32[784,4096]{1,0:T(8,128)S(1)}) fusion(f32[784,4096]{1,0:T(8,128)} %fusion.97, f32[4096]{0:T(1024)S(1)} %bitcast.176, bf16[784,1024]{1,0:T(8,128)(2,1)S(1)} %copy-done.22, bf16[4096,1024]{1,0:T(8,128)(2,1)} %all-gather.8.cloned.1.call-done), kind=kOutput, calls=%fused_computation.12 | convolution fusion | flops 6817509376 | bytes 42139648 | tf_op jit(solution)/shard_map/dot_general | solution.py:36
  299.5 15.3 %reshape.497 = bf16[784,2,2,1024]{3,2,1,0:T(2,128)(2,1)} reshape(bf16[784,4096]{1,0:T(8,128)(2,1)} %multiply_convert_fusion.1) | data formatting | bytes 12845056 | tf_op jit(solution)/shard_map/reshape | solution.py:394
  314.8 55.2 %dynamic-slice_reduce_fusion.1 = bf16[784,2,1024]{2,1,0:T(2,128)(2,1)} fusion(bf16[784,2,2,1024]{3,2,1,0:T(2,128)(2,1)} %reshape.497, s32[]{:T(128)S(6)} %select_n.557), kind=kLoop, calls=%fused_computation.31 | loop fusion | bytes 6422532 | tf_op jit(solution)/shard_map/jit(dynamic_index_in_dim)/dynamic_slice | solution.py:395
  369.9 53.9 %dynamic-slice_reduce_fusion = bf16[784,2,1024]{2,1,0:T(2,128)(2,1)} fusion(bf16[784,2,2,1024]{3,2,1,0:T(2,128)(2,1)S(1)} %copy-done.2, s32[]{:T(128)S(6)} %select_n.572), kind=kLoop, calls=%fused_computation.30 | loop fusion | bytes 6422532 | tf_op jit(solution)/shard_map/jit(dynamic_index_in_dim)/dynamic_slice | solution.py:395
  423.8 15.4 %reshape.494 = bf16[784,2,2,1024]{3,2,1,0:T(2,128)(2,1)} reshape(bf16[784,4096]{1,0:T(8,128)(2,1)} %get-tuple-element.53) | data formatting | bytes 12845056 | tf_op jit(solution)/shard_map/reshape | solution.py:394
  439.2 55.4 %dynamic-slice_reduce_fusion.3 = bf16[784,2,1024]{2,1,0:T(2,128)(2,1)} fusion(bf16[784,2,2,1024]{3,2,1,0:T(2,128)(2,1)} %reshape.494, s32[]{:T(128)S(6)} %select_n.557), kind=kLoop, calls=%fused_computation.33 | loop fusion | bytes 6422532 | tf_op jit(solution)/shard_map/jit(dynamic_index_in_dim)/dynamic_slice | solution.py:395
  494.6 53.7 %dynamic-slice_reduce_fusion.2 = bf16[784,2,1024]{2,1,0:T(2,128)(2,1)} fusion(bf16[784,2,2,1024]{3,2,1,0:T(2,128)(2,1)S(1)} %copy-done.3, s32[]{:T(128)S(6)} %select_n.572), kind=kLoop, calls=%fused_computation.32 | loop fusion | bytes 6422532 | tf_op jit(solution)/shard_map/jit(dynamic_index_in_dim)/dynamic_slice | solution.py:395
  548.4 10.5 multiply_reduce_fusion.2
  583.2 12.6 add_convert_fusion.2
  611.3 29.9 %fusion.31 = bf16[8,64,1568]{2,1,0:T(8,128)(2,1)} fusion(f32[8,1568,1568]{1,2,0:T(8,128)} %get-tuple-element.134, f32[8,1568]{1,0:T(8,128)S(1)} %copy-done.9, bf16[784,8,64]{0,2,1:T(8,128)(2,1)S(1)} %bitcast.140, bf16[784,8,64]{0,2,1:T(8,128)(2,1)S(1)} %bitcast.138), kind=kOutput, calls=%fused_computation.87 | convolution fusion | flops 2580652032 | bytes 81937408 | tf_op jit(solution)/shard_map/hqk,qhd->khd/dot_general | solution.py:91
  641.1 58.2 %multiply_reduce_fusion = (f32[8,1568]{1,0:T(8,128)S(1)}, f32[8,1568,1568]{1,2,0:T(8,128)}) fusion(f32[8,1568,1568]{1,2,0:T(8,128)} %get-tuple-element.134, f32[8,1568]{1,0:T(8,128)S(1)} %copy-done.9, bf16[1568,8,64]{0,2,1:T(8,128)(2,1)} %bitcast.146, bf16[784,8,64]{0,2,1:T(8,128)(2,1)S(1)} %bitcast.141, bf16[784,8,64]{0,2,1:T(8,128)(2,1)S(1)} %bitcast.139), kind=kOutput, calls=%fused_computation.1 | convolution fusion | flops 2599505664 | bytes 160663552 | tf_op jit(solution)/shard_map/qhd,khd->hqk/dot_general | solution.py:88
  699.3 64.9 %multiply_convert_fusion = bf16[8,1568,1568]{1,2,0:T(8,128)(2,1)} fusion(f32[8,1568,1568]{1,2,0:T(8,128)} %get-tuple-element.139, f32[8,1568,1568]{1,2,0:T(8,128)} %get-tuple-element.134, f32[8,1568]{1,0:T(8,128)S(1)} %get-tuple-element.138, f32[8,1568]{1,0:T(8,128)S(1)} %copy-done.9), kind=kLoop, calls=%fused_computation | loop fusion | flops 98344960 | bytes 196790272 | tf_op jit(solution)/shard_map/convert_element_type | solution.py:93
  764.3 20.1 %multiply_convert_fusion.2 = bf16[8,64,1568]{2,1,0:T(8,128)(2,1)} fusion(bf16[1568,8,64]{0,2,1:T(8,128)(2,1)S(1)} %bitcast.126, bf16[8,1568,1568]{1,2,0:T(8,128)(2,1)} %multiply_convert_fusion), kind=kOutput, calls=%fused_computation.59 | convolution fusion | flops 2519236608 | bytes 42549248 | tf_op jit(solution)/shard_map/hqk,qhd->khd/dot_general | solution.py:99
  784.3 17.5 %multiply_convert_fusion.3 = bf16[8,64,1568]{2,1,0:T(8,128)(2,1)} fusion(bf16[1568,8,64]{0,2,1:T(8,128)(2,1)S(1)} %bitcast.124, bf16[8,1568,1568]{1,2,0:T(8,128)(2,1)} %multiply_convert_fusion), kind=kOutput, calls=%fused_computation.60 | convolution fusion | flops 2519236608 | bytes 42549248 | tf_op jit(solution)/shard_map/hqk,khd->qhd/dot_general | solution.py:95
  821.8 36.2 %collective-permute-done.20 = bf16[256,1024]{1,0:T(8,128)(2,1)S(1)} collective-permute-done((bf16[256,1024]{1,0:T(8,128)(2,1)S(1)}, bf16[256,1024]{1,0:T(8,128)(2,1)S(1)}, u32[]{:S(2)}, u32[]{:S(2)}) %collective-permute-start.20) | collective-permute-done | bytes 524320 | tf_op jit(solution)/shard_map/ppermute | solution.py:383
  884.9 38.8 %all-reduce = (f32[4096]{0:T(1024)S(1)}, f32[8192]{0:T(1024)S(1)}) all-reduce(f32[4096]{0:T(1024)S(1)} %pad_maximum_fusion.38, f32[8192]{0:T(1024)S(1)} %copy-done.40), channel_id=1, replica_groups=mesh['rep'=16,'grp'=2] {'rep','grp'}, use_global_device_ids=true, to_apply=%region_14.15 | all-reduce | flops 12288 | bytes 98304 | tf_op jit(solution)/shard_map/psum | solution.py:590
  969.3 28.4 %collective-permute-done.30 = bf16[512,2048]{1,0:T(8,128)(2,1)S(1)} collective-permute-done((bf16[512,2048]{1,0:T(8,128)(2,1)S(1)}, bf16[512,2048]{1,0:T(8,128)(2,1)S(1)}, u32[]{:S(2)}, u32[]{:S(2)}) %collective-permute-start.30) | collective-permute-done | bytes 2097184 | tf_op jit(solution)/shard_map/ppermute | solution.py:383
  1006.9 34.9 %collective-permute-done.40 = bf16[1024,1024]{1,0:T(8,128)(2,1)S(1)} collective-permute-done((bf16[1024,1024]{1,0:T(8,128)(2,1)S(1)}, bf16[1024,1024]{1,0:T(8,128)(2,1)S(1)}, u32[]{:S(2)}, u32[]{:S(2)}) %collective-permute-start.40) | collective-permute-done | bytes 2097184 | tf_op jit(solution)/shard_map/ppermute | solution.py:383
  1050.9 19.6 %collective-permute-done.41 = bf16[512,1024]{1,0:T(8,128)(2,1)S(1)} collective-permute-done((bf16[512,1024]{1,0:T(8,128)(2,1)S(1)}, bf16[512,1024]{1,0:T(8,128)(2,1)S(1)}, u32[]{:S(2)}, u32[]{:S(2)}) %collective-permute-start.41) | collective-permute-done | bytes 1048608 | tf_op jit(solution)/shard_map/ppermute | solution.py:383
  1073.5 15.3 %collective-permute-done.42 = bf16[256,1024]{1,0:T(8,128)(2,1)S(1)} collective-permute-done((bf16[256,1024]{1,0:T(8,128)(2,1)S(1)}, bf16[256,1024]{1,0:T(8,128)(2,1)S(1)}, u32[]{:S(2)}, u32[]{:S(2)}) %collective-permute-start.42) | collective-permute-done | bytes 524320 | tf_op jit(solution)/shard_map/ppermute | solution.py:383
  1092.2 14.6 %collective-permute-done.43 = bf16[128,1024]{1,0:T(8,128)(2,1)S(1)} collective-permute-done((bf16[128,1024]{1,0:T(8,128)(2,1)S(1)}, bf16[128,1024]{1,0:T(8,128)(2,1)S(1)}, u32[]{:S(2)}, u32[]{:S(2)}) %collective-permute-start.43) | collective-permute-done | bytes 262176 | tf_op jit(solution)/shard_map/ppermute | solution.py:383
  1107.0 11.1 collective-permute-done.34
  1123.9 11.1 collective-permute-done.35
  1146.5 14.9 %collective-permute-done.36 = bf16[256,2048]{1,0:T(8,128)(2,1)S(1)} collective-permute-done((bf16[256,2048]{1,0:T(8,128)(2,1)S(1)}, bf16[256,2048]{1,0:T(8,128)(2,1)S(1)}, u32[]{:S(2)}, u32[]{:S(2)}) %collective-permute-start.36) | collective-permute-done | bytes 1048608 | tf_op jit(solution)/shard_map/ppermute | solution.py:383
  1165.4 17.4 %collective-permute-done.46 = bf16[512,1024]{1,0:T(8,128)(2,1)S(1)} collective-permute-done((bf16[512,1024]{1,0:T(8,128)(2,1)S(1)}, bf16[512,1024]{1,0:T(8,128)(2,1)S(1)}, u32[]{:S(2)}, u32[]{:S(2)}) %collective-permute-start.46) | collective-permute-done | bytes 1048608 | tf_op jit(solution)/shard_map/ppermute | solution.py:383
  (435 shorter events, 376.9 us)
Async XLA Ops:
  7.2 227.1 %all-gather.4.cloned.1.call-start = ((), (), s32[]{:S(2)}) async-start(), calls=%async_computation | async-start | bytes 2162688 | tf_op jit(solution)/shard_map/all_gather | solution.py:496
  11.8 229.8 %all-gather.6.cloned.1.call-start = ((), (), s32[]{:S(2)}) async-start(), calls=%async_computation.1 | async-start | bytes 8650752 | tf_op jit(solution)/shard_map/all_gather | solution.py:496
  13.8 241.7 %all-gather.8.cloned.1.call-start = ((), (), s32[]{:S(2)}) async-start(), calls=%async_computation.2 | async-start | bytes 8650752 | tf_op jit(solution)/shard_map/all_gather | solution.py:496
  34.3 44.3 %collective-permute-start.3 = (bf16[256,1536]{1,0:T(8,128)(2,1)S(1)}, bf16[256,1536]{1,0:T(8,128)(2,1)S(1)}, u32[]{:S(2)}, u32[]{:S(2)}) collective-permute-start(bf16[256,1536]{1,0:T(8,128)(2,1)S(1)} %constant_dynamic-slice_fusion.6), channel_id=1, source_target_pairs={{0,1},{1,0},{2,3},{3,2},{4,5},{5,4},{6,7},{7,6},{8,9},{9,8},{10,11... | collective-permute-start | bytes 2359304 | tf_op jit(solution)/shard_map/ppermute | solution.py:383
  82.7 135.2 %collective-permute-start.7 = (bf16[784,1024]{1,0:T(8,128)(2,1)}, bf16[784,1024]{1,0:T(8,128)(2,1)}, u32[]{:S(2)}, u32[]{:S(2)}) collective-permute-start(bf16[784,1024]{1,0:T(8,128)(2,1)} %bitcast.170), channel_id=1, source_target_pairs={{1,2},{2,1},{5,6},{6,5},{9,10},{10,9},{13,14},{14,13},{17,18},{18,... | collective-permute-start | bytes 4816904 | tf_op jit(solution)/shard_map/ppermute | solution.py:443
  240.7 697.4 %collective-permute-start.28 = (bf16[784,1024]{1,0:T(8,128)(2,1)}, bf16[784,1024]{1,0:T(8,128)(2,1)}, u32[]{:S(2)}, u32[]{:S(2)}) collective-permute-start(bf16[784,1024]{1,0:T(8,128)(2,1)} %add_convert_fusion.3), channel_id=1, source_target_pairs={{0,2},{2,0},{4,6},{6,4},{8,10},{10,8},{12,14},{14,12},{16,18},{18,... | collective-permute-start | bytes 4816904 | tf_op jit(solution)/shard_map/ppermute | solution.py:383
  561.8 253.8 %collective-permute-start.19 = (bf16[784,1024]{1,0:T(8,128)(2,1)}, bf16[784,1024]{1,0:T(8,128)(2,1)}, u32[]{:S(2)}, u32[]{:S(2)}) collective-permute-start(bf16[784,1024]{1,0:T(8,128)(2,1)} %get-tuple-element.56), channel_id=1, source_target_pairs={{0,2},{2,0},{4,6},{6,4},{8,10},{10,8},{12,14},{14,12},{16,18},{18,... | collective-permute-start | bytes 4816904 | tf_op jit(solution)/shard_map/ppermute | solution.py:383
  582.8 27.9 %collective-permute-start.8 = (bf16[784,512]{1,0:T(8,128)(2,1)S(1)}, bf16[784,512]{1,0:T(8,128)(2,1)S(1)}, u32[]{:S(2)}, u32[]{:S(2)}) collective-permute-start(bf16[784,512]{1,0:T(8,128)(2,1)S(1)} %bitcast.171), channel_id=1, source_target_pairs={{0,2},{2,0},{4,6},{6,4},{8,10},{10,8},{12,14},{14,12},{16,18},{18,... | collective-permute-start | bytes 2408456 | tf_op jit(solution)/shard_map/ppermute | solution.py:383
  595.8 223.1 %collective-permute-start.6 = (bf16[784,1024]{1,0:T(8,128)(2,1)}, bf16[784,1024]{1,0:T(8,128)(2,1)}, u32[]{:S(2)}, u32[]{:S(2)}) collective-permute-start(bf16[784,1024]{1,0:T(8,128)(2,1)} %add_convert_fusion.2), channel_id=1, source_target_pairs={{1,2},{2,1},{5,6},{6,5},{9,10},{10,9},{13,14},{14,13},{17,18},{18,... | collective-permute-start | bytes 4816904 | tf_op jit(solution)/shard_map/ppermute | solution.py:443
  602.1 344.6 %collective-permute-start.38 = (bf16[784,2048]{1,0:T(8,128)(2,1)}, bf16[784,2048]{1,0:T(8,128)(2,1)}, u32[]{:S(2)}, u32[]{:S(2)}) collective-permute-start(bf16[784,2048]{1,0:T(8,128)(2,1)} %bitcast.77), channel_id=1, source_target_pairs={{0,2},{2,0},{4,6},{6,4},{8,10},{10,8},{12,14},{14,12},{16,18},{18,... | collective-permute-start | bytes 9633800 | tf_op jit(solution)/shard_map/ppermute | solution.py:383
  809.8 51.4 %collective-permute-start.11 = (bf16[512,1536]{1,0:T(8,128)(2,1)S(1)}, bf16[512,1536]{1,0:T(8,128)(2,1)S(1)}, u32[]{:S(2)}, u32[]{:S(2)}) collective-permute-start(bf16[512,1536]{1,0:T(8,128)(2,1)S(1)} %convolution_convert_fusion.1), channel_id=1, source_target_pairs={{0,1},{1,0},{2,3},{3,2},{4,5},{5,4},{6,7},{7,6},{8,9},{9,8},{10,11... | collective-permute-start | bytes 4718600 | tf_op jit(solution)/shard_map/ppermute | solution.py:383
  818.6 39.4 %collective-permute-start.20 = (bf16[256,1024]{1,0:T(8,128)(2,1)S(1)}, bf16[256,1024]{1,0:T(8,128)(2,1)S(1)}, u32[]{:S(2)}, u32[]{:S(2)}) collective-permute-start(bf16[256,1024]{1,0:T(8,128)(2,1)S(1)} %fusion.60), channel_id=1, source_target_pairs={{0,1},{1,0},{2,3},{3,2},{4,5},{5,4},{6,7},{7,6},{8,9},{9,8},{10,11... | collective-permute-start | bytes 1572872 | tf_op jit(solution)/shard_map/ppermute | solution.py:383
  818.9 112.6 %collective-permute-start.29 = (bf16[784,2048]{1,0:T(8,128)(2,1)}, bf16[784,2048]{1,0:T(8,128)(2,1)}, u32[]{:S(2)}, u32[]{:S(2)}) collective-permute-start(bf16[784,2048]{1,0:T(8,128)(2,1)} %bitcast.73), channel_id=1, source_target_pairs={{0,2},{2,0},{4,6},{6,4},{8,10},{10,8},{12,14},{14,12},{16,18},{18,... | collective-permute-start | bytes 9633800 | tf_op jit(solution)/shard_map/ppermute | solution.py:383
  870.0 58.9 %collective-permute-start.12 = (bf16[256,1536]{1,0:T(8,128)(2,1)S(1)}, bf16[256,1536]{1,0:T(8,128)(2,1)}, u32[]{:S(2)}, u32[]{:S(2)}) collective-permute-start(bf16[256,1536]{1,0:T(8,128)(2,1)S(1)} %dynamic-slice_convert_fusion.2), channel_id=1, source_target_pairs={{0,4},{2,6},{4,0},{6,2},{8,12},{10,14},{12,8},{14,10},{16,20},{18,... | collective-permute-start | bytes 2359304 | tf_op jit(solution)/shard_map/ppermute | solution.py:383
  883.0 40.7 %collective-permute-start.24 = (bf16[32,1024]{1,0:T(8,128)(2,1)S(1)}, bf16[32,1024]{1,0:T(8,128)(2,1)S(1)}, u32[]{:S(2)}, u32[]{:S(2)}) collective-permute-start(bf16[32,1024]{1,0:T(8,128)(2,1)S(1)} %add_convert_fusion.7), channel_id=1, source_target_pairs={{0,16},{2,18},{4,20},{6,22},{8,24},{10,26},{12,28},{14,30},{16,0},... | collective-permute-start | bytes 196616 | tf_op jit(solution)/shard_map/ppermute | solution.py:383
  928.8 23.7 %collective-permute-start.39 = (bf16[784,1024]{1,0:T(8,128)(2,1)S(1)}, bf16[784,1024]{1,0:T(8,128)(2,1)S(1)}, u32[]{:S(2)}, u32[]{:S(2)}) collective-permute-start(bf16[784,1024]{1,0:T(8,128)(2,1)S(1)} %copy-done.24), channel_id=1, source_target_pairs={{0,2},{2,0},{4,6},{6,4},{8,10},{10,8},{12,14},{14,12},{16,18},{18,... | collective-permute-start | bytes 4816904 | tf_op jit(solution)/shard_map/ppermute | solution.py:383
  928.9 256.2 %collective-permute-start.10 = (bf16[784,1024]{1,0:T(8,128)(2,1)}, bf16[784,1024]{1,0:T(8,128)(2,1)S(1)}, u32[]{:S(2)}, u32[]{:S(2)}) collective-permute-start(bf16[784,1024]{1,0:T(8,128)(2,1)} %fusion.23), channel_id=1, source_target_pairs={{1,2},{2,1},{5,6},{6,5},{9,10},{10,9},{13,14},{14,13},{17,18},{18,... | collective-permute-start | bytes 4816904 | tf_op jit(solution)/shard_map/ppermute | solution.py:443
  931.6 26.9 %collective-permute-start.26 = (bf16[128,1024]{1,0:T(8,128)(2,1)S(1)}, bf16[128,1024]{1,0:T(8,128)(2,1)S(1)}, u32[]{:S(2)}, u32[]{:S(2)}) collective-permute-start(bf16[128,1024]{1,0:T(8,128)(2,1)S(1)} %pad_maximum_fusion.36), channel_id=1, source_target_pairs={{0,4},{2,6},{4,0},{6,2},{8,12},{10,14},{12,8},{14,10},{16,20},{18,... | collective-permute-start | bytes 786440 | tf_op jit(solution)/shard_map/ppermute | solution.py:383
  946.7 51.0 %collective-permute-start.30 = (bf16[512,2048]{1,0:T(8,128)(2,1)S(1)}, bf16[512,2048]{1,0:T(8,128)(2,1)S(1)}, u32[]{:S(2)}, u32[]{:S(2)}) collective-permute-start(bf16[512,2048]{1,0:T(8,128)(2,1)S(1)} %convolution_convert_fusion), channel_id=1, source_target_pairs={{0,1},{1,0},{2,3},{3,2},{4,5},{5,4},{6,7},{7,6},{8,9},{9,8},{10,11... | collective-permute-start | bytes 6291464 | tf_op jit(solution)/shard_map/ppermute | solution.py:383
  957.0 84.8 %collective-permute-start.40 = (bf16[1024,1024]{1,0:T(8,128)(2,1)S(1)}, bf16[1024,1024]{1,0:T(8,128)(2,1)S(1)}, u32[]{:S(2)}, u32[]{:S(2)}) collective-permute-start(bf16[1024,1024]{1,0:T(8,128)(2,1)S(1)} %fusion.41), channel_id=1, source_target_pairs={{0,1},{1,0},{2,3},{3,2},{4,5},{5,4},{6,7},{7,6},{8,9},{9,8},{10,11... | collective-permute-start | bytes 6291464 | tf_op jit(solution)/shard_map/ppermute | solution.py:383
  958.6 204.9 %collective-permute-start.27 = (bf16[256,1024]{1,0:T(8,128)(2,1)S(1)}, bf16[256,1024]{1,0:T(8,128)(2,1)S(1)}, u32[]{:S(2)}, u32[]{:S(2)}) collective-permute-start(bf16[256,1024]{1,0:T(8,128)(2,1)S(1)} %pad_maximum_fusion.32), channel_id=1, source_target_pairs={{0,2},{2,0},{4,6},{6,4},{8,10},{10,8},{12,14},{14,12},{16,18},{18,... | collective-permute-start | bytes 1572872 | tf_op jit(solution)/shard_map/ppermute | solution.py:383
  969.2 79.2 %collective-permute-start.15 = (bf16[64,1536]{1,0:T(8,128)(2,1)S(1)}, bf16[64,1536]{1,0:T(8,128)(2,1)S(1)}, u32[]{:S(2)}, u32[]{:S(2)}) collective-permute-start(bf16[64,1536]{1,0:T(8,128)(2,1)S(1)} %add_convert_fusion.6), channel_id=1, source_target_pairs={{0,16},{2,18},{4,20},{6,22},{8,24},{10,26},{12,28},{14,30},{16,0},... | collective-permute-start | bytes 589832 | tf_op jit(solution)/shard_map/ppermute | solution.py:383
  1003.3 45.1 %collective-permute-start.31 = (bf16[256,2048]{1,0:T(8,128)(2,1)S(1)}, bf16[256,2048]{1,0:T(8,128)(2,1)S(1)}, u32[]{:S(2)}, u32[]{:S(2)}) collective-permute-start(bf16[256,2048]{1,0:T(8,128)(2,1)S(1)} %dynamic-slice_convert_fusion.1), channel_id=1, source_target_pairs={{0,4},{2,6},{4,0},{6,2},{8,12},{10,14},{12,8},{14,10},{16,20},{18,... | collective-permute-start | bytes 3145736 | tf_op jit(solution)/shard_map/ppermute | solution.py:383
  1046.1 24.5 %collective-permute-start.41 = (bf16[512,1024]{1,0:T(8,128)(2,1)S(1)}, bf16[512,1024]{1,0:T(8,128)(2,1)S(1)}, u32[]{:S(2)}, u32[]{:S(2)}) collective-permute-start(bf16[512,1024]{1,0:T(8,128)(2,1)S(1)} %dynamic-slice_convert_fusion), channel_id=1, source_target_pairs={{0,4},{2,6},{4,0},{6,2},{8,12},{10,14},{12,8},{14,10},{16,20},{18,... | collective-permute-start | bytes 3145736 | tf_op jit(solution)/shard_map/ppermute | solution.py:383
  1048.7 23.3 %collective-permute-start.32 = (bf16[128,2048]{1,0:T(8,128)(2,1)S(1)}, bf16[128,2048]{1,0:T(8,128)(2,1)S(1)}, u32[]{:S(2)}, u32[]{:S(2)}) collective-permute-start(bf16[128,2048]{1,0:T(8,128)(2,1)S(1)} %dynamic-slice_convert_fusion.4), channel_id=1, source_target_pairs={{0,8},{2,10},{4,12},{6,14},{8,0},{10,2},{12,4},{14,6},{16,24},{18,... | collective-permute-start | bytes 1572872 | tf_op jit(solution)/shard_map/ppermute | solution.py:383
  1050.1 42.0 %collective-permute-start.16 = (bf16[128,1536]{1,0:T(8,128)(2,1)S(1)}, bf16[128,1536]{1,0:T(8,128)(2,1)S(1)}, u32[]{:S(2)}, u32[]{:S(2)}) collective-permute-start(bf16[128,1536]{1,0:T(8,128)(2,1)S(1)} %pad_maximum_fusion.35), channel_id=1, source_target_pairs={{0,8},{2,10},{4,12},{6,14},{8,0},{10,2},{12,4},{14,6},{16,24},{18,... | collective-permute-start | bytes 1179656 | tf_op jit(solution)/shard_map/ppermute | solution.py:383
  1089.1 29.0 %collective-permute-start.34 = (bf16[64,2048]{1,0:T(8,128)(2,1)S(1)}, bf16[64,2048]{1,0:T(8,128)(2,1)S(1)}, u32[]{:S(2)}, u32[]{:S(2)}) collective-permute-start(bf16[64,2048]{1,0:T(8,128)(2,1)S(1)} %add_convert_fusion.5), channel_id=1, source_target_pairs={{0,16},{2,18},{4,20},{6,22},{8,24},{10,26},{12,28},{14,30},{16,0},... | collective-permute-start | bytes 786440 | tf_op jit(solution)/shard_map/ppermute | solution.py:383
  1135.2 26.1 %collective-permute-start.36 = (bf16[256,2048]{1,0:T(8,128)(2,1)S(1)}, bf16[256,2048]{1,0:T(8,128)(2,1)S(1)}, u32[]{:S(2)}, u32[]{:S(2)}) collective-permute-start(bf16[256,2048]{1,0:T(8,128)(2,1)S(1)} %pad_maximum_fusion.24), channel_id=1, source_target_pairs={{0,4},{2,6},{4,0},{6,2},{8,12},{10,14},{12,8},{14,10},{16,20},{18,... | collective-permute-start | bytes 3145736 | tf_op jit(solution)/shard_map/ppermute | solution.py:383
  1138.1 49.7 %collective-permute-start.18 = (bf16[512,1536]{1,0:T(8,128)(2,1)S(1)}, bf16[512,1536]{1,0:T(8,128)(2,1)S(1)}, u32[]{:S(2)}, u32[]{:S(2)}) collective-permute-start(bf16[512,1536]{1,0:T(8,128)(2,1)S(1)} %pad_maximum_fusion.6), channel_id=1, source_target_pairs={{0,2},{2,0},{4,6},{6,4},{8,10},{10,8},{12,14},{14,12},{16,18},{18,... | collective-permute-start | bytes 4718600 | tf_op jit(solution)/shard_map/ppermute | solution.py:383
  1146.4 36.4 %collective-permute-start.46 = (bf16[512,1024]{1,0:T(8,128)(2,1)S(1)}, bf16[512,1024]{1,0:T(8,128)(2,1)S(1)}, u32[]{:S(2)}, u32[]{:S(2)}) collective-permute-start(bf16[512,1024]{1,0:T(8,128)(2,1)S(1)} %pad_maximum_fusion.25), channel_id=1, source_target_pairs={{0,4},{2,6},{4,0},{6,2},{8,12},{10,14},{12,8},{14,10},{16,20},{18,... | collective-permute-start | bytes 3145736 | tf_op jit(solution)/shard_map/ppermute | solution.py:383
  1163.5 76.0 %collective-permute-start.37 = (bf16[512,2048]{1,0:T(8,128)(2,1)}, bf16[512,2048]{1,0:T(8,128)(2,1)}, u32[]{:S(2)}, u32[]{:S(2)}) collective-permute-start(bf16[512,2048]{1,0:T(8,128)(2,1)} %pad_maximum_fusion.7), channel_id=1, source_target_pairs={{0,2},{2,0},{4,6},{6,4},{8,10},{10,8},{12,14},{14,12},{16,18},{18,... | collective-permute-start | bytes 6291464 | tf_op jit(solution)/shard_map/ppermute | solution.py:383
  1185.1 98.9 %collective-permute-start.47 = (bf16[1024,1024]{1,0:T(8,128)(2,1)}, bf16[1024,1024]{1,0:T(8,128)(2,1)}, u32[]{:S(2)}, u32[]{:S(2)}) collective-permute-start(bf16[1024,1024]{1,0:T(8,128)(2,1)} %pad_maximum_fusion.8), channel_id=1, source_target_pairs={{0,2},{2,0},{4,6},{6,4},{8,10},{10,8},{12,14},{14,12},{16,18},{18,... | collective-permute-start | bytes 6291464 | tf_op jit(solution)/shard_map/ppermute | solution.py:383
  (90 other events, 1854.4 us)
Sparse Core Ops, SparseCore 0:
  12.0 81.9 all-gather.3
  97.4 76.8 all-gather.5
  177.7 75.6 all-gather.7
